TPU v7x, 32 devices: a whole 2x2x4 slice. The times are simulated.
32 devices in a mesh: mem: 4 (over z), lat: 8 (over y, x, core).
Axes of the slice: x: 2, y: 2, z: 4, core: 2. Of those that a mesh axis runs over, the one named last changes fastest.
Arguments:
- features: bfloat16 [16, 16, 1440, 128], P('mem', 'lat'), may hold values from -6 to 6
- conv_inner: bfloat16 [3, 3, 128, 128], replicated, may hold values from -0.1875 to 0.1875
- conv_head: bfloat16 [3, 3, 128, 69], replicated, may hold values from -0.1875 to 0.1875
- truth: float32 [69, 16, 1440], P(None, 'lat'), may hold values from -5 to 5
- kernel_width: float32 [69], replicated, may hold values from 0.3 to 1.5
- var_weight: float32 [69], replicated, may hold values from 0.5 to 2
Outputs:
- grad_features: bfloat16 [16, 16, 1440, 128], P('mem', 'lat')
- grad_inner: float32 [3, 3, 128, 128], replicated
- grad_head: float32 [3, 3, 128, 69], replicated
All inputs are finite; a program needn't handle non-finite values.
Results may differ from a plain program's by a relative error of at most 0.0098.
Values may be sent and summed in bfloat16 or wider, within the bound.
No kernel may reach another device: no remote copies, remote signals or barrier semaphores. Data moves between devices by JAX's collectives and lax.ppermute only.
A program may use at most 256 MiB of HBM per device.

v0:
```python
import jax
import jax.numpy as jnp
from jax import lax
from jax.sharding import PartitionSpec as P


def padded_2(cells, sides, width):
    for axis, dim in sides:
        count = lax.axis_size(axis)
        ends = count - 1
        head = lax.slice_in_dim(cells, 0, width, axis=dim)
        tail = lax.slice_in_dim(cells, cells.shape[dim] - width, cells.shape[dim], axis=dim)
        cells = jnp.concatenate(
            [
                lax.ppermute(tail, axis, [(i, (i + 1) % count) for i in range(ends)]),
                cells,
                lax.ppermute(head, axis, [((i + 1) % count, i) for i in range(ends)]),
            ],
            axis=dim,
        )
    return cells


def wrap_lon(values, axis):
    count = values.shape[axis]
    return jnp.concatenate(
        [
            lax.slice_in_dim(values, count - 1, count, axis=axis),
            values,
            lax.slice_in_dim(values, 0, 1, axis=axis),
        ],
        axis=axis,
    )


def gelu_slope(pre):
    return jax.jvp(jax.nn.gelu, (pre,), (jnp.ones_like(pre),))[1]


def hidden_conv(padded, kernel, band_rows):
    lon_cells = padded.shape[2] - 2
    summed = jnp.zeros((padded.shape[0], band_rows, lon_cells, kernel.shape[3]), jnp.float32)
    for row_off in range(3):
        for col_off in range(3):
            summed = summed + jnp.einsum(
                "mrlc,co->mrlo",
                padded[:, row_off : row_off + band_rows, col_off : col_off + lon_cells],
                kernel[row_off, col_off],
                preferred_element_type=jnp.float32,
            )
    return summed


def field_conv(padded, kernel, band_rows):
    lon_cells = padded.shape[2] - 2
    summed = jnp.zeros((padded.shape[0], kernel.shape[3], band_rows, lon_cells), jnp.float32)
    for row_off in range(3):
        for col_off in range(3):
            summed = summed + jnp.einsum(
                "mrlc,cv->mvrl",
                padded[:, row_off : row_off + band_rows, col_off : col_off + lon_cells],
                kernel[row_off, col_off],
                preferred_element_type=jnp.float32,
            )
    return summed


def field_back(padded_grad, kernel, band_rows):
    lon_cells = padded_grad.shape[3] - 2
    summed = jnp.zeros((padded_grad.shape[0], band_rows, lon_cells, kernel.shape[2]), jnp.float32)
    for row_off in range(3):
        for col_off in range(3):
            summed = summed + jnp.einsum(
                "mvrl,cv->mrlc",
                padded_grad[
                    :,
                    :,
                    2 - row_off : 2 - row_off + band_rows,
                    2 - col_off : 2 - col_off + lon_cells,
                ],
                kernel[row_off, col_off],
                preferred_element_type=jnp.float32,
            )
    return summed


def hidden_back(padded_grad, kernel, band_rows):
    lon_cells = padded_grad.shape[2] - 2
    summed = jnp.zeros((padded_grad.shape[0], band_rows, lon_cells, kernel.shape[2]), jnp.float32)
    for row_off in range(3):
        for col_off in range(3):
            summed = summed + jnp.einsum(
                "mrlo,co->mrlc",
                padded_grad[
                    :, 2 - row_off : 2 - row_off + band_rows, 2 - col_off : 2 - col_off + lon_cells
                ],
                kernel[row_off, col_off],
                preferred_element_type=jnp.float32,
            )
    return summed


def kernel_grad(padded_input, grad_out, form, band_rows, lon_cells):
    pieces = []
    for row_off in range(3):
        for col_off in range(3):
            pieces.append(
                jnp.einsum(
                    form,
                    padded_input[:, row_off : row_off + band_rows, col_off : col_off + lon_cells],
                    grad_out,
                    preferred_element_type=jnp.float32,
                )
            )
    return jnp.stack(pieces).reshape((3, 3) + pieces[0].shape)


def pair_sums(own, others, inverse):
    spread = others[None] - own[:, None]
    kernel = jnp.exp(-0.5 * spread * spread * inverse[None, None, :, None, None])
    return jnp.sum(kernel * spread, axis=1)


def member_grad(own, pairwise, truth_piece, inverse, var_weight, members):
    offset = own - truth_piece[None]
    nearness = jnp.exp(-0.5 * offset * offset * inverse[None, :, None, None])
    scale = (var_weight * inverse)[None, :, None, None]
    return scale * (2.0 / (members - 1) * pairwise + 2.0 * nearness * offset)


def split_groups(values, blocks, group):
    shaped = values.reshape((values.shape[0], blocks, group) + values.shape[2:])
    return jnp.moveaxis(shaped, 1, 0)


def shards(features, conv_inner, conv_head, truth, kernel_width, var_weight):
    band_rows = features.shape[1]
    lon_cells = features.shape[2]
    variables = conv_head.shape[3]
    feature_ext = padded_2(features, (("lat", 1),), 1)
    pre_own = hidden_conv(wrap_lon(feature_ext, 2), conv_inner, band_rows)
    hidden_own = jax.nn.gelu(pre_own).astype(jnp.bfloat16)
    hidden_ext = padded_2(hidden_own, (("lat", 1),), 1)
    hidden_wrap = wrap_lon(hidden_ext, 2)
    field = field_conv(hidden_wrap, conv_head, band_rows).astype(jnp.bfloat16)
    inverse = 1.0 / (kernel_width * kernel_width)
    group = 3
    blocks = variables // group
    inverse_blocks = inverse.reshape(blocks, group)
    gathered = lax.all_to_all(field, "mem", split_axis=3, concat_axis=0, tiled=True)
    values = gathered.astype(jnp.float32)
    members = values.shape[0]
    piece_cells = values.shape[3]

    def block_pairs(packed):
        member_values, rates = packed
        return pair_sums(member_values, member_values, rates)

    pairwise = lax.map(block_pairs, (split_groups(values, blocks, group), inverse_blocks))
    pairwise = jnp.moveaxis(pairwise, 0, 1).reshape(values.shape)
    truth_piece = lax.dynamic_slice_in_dim(
        truth, lax.axis_index("mem") * piece_cells, piece_cells, 2
    )
    gradient = member_grad(values, pairwise, truth_piece, inverse, var_weight, members).astype(
        jnp.bfloat16
    )
    field_grad = lax.all_to_all(gradient, "mem", split_axis=0, concat_axis=3, tiled=True)
    grad_pad = padded_2(field_grad, (("lat", 2),), 1)
    hidden_grad = (
        field_back(wrap_lon(grad_pad, 3), conv_head, band_rows) * gelu_slope(pre_own)
    ).astype(jnp.bfloat16)
    head_grad = kernel_grad(hidden_wrap, field_grad, "mrlc,mvrl->cv", band_rows, lon_cells)
    hidden_pad = padded_2(hidden_grad, (("lat", 1),), 1)
    grad_features = hidden_back(wrap_lon(hidden_pad, 2), conv_inner, band_rows).astype(jnp.bfloat16)
    inner_grad = kernel_grad(
        wrap_lon(feature_ext, 2), hidden_grad, "mrlc,mrlo->co", band_rows, lon_cells
    )
    inner_sum, head_sum = lax.psum((inner_grad, head_grad), ("mem", "lat"))
    points = band_rows * lax.axis_size("lat") * lon_cells
    return (grad_features, inner_sum / points, head_sum / points)


def solution(mesh):
    in_specs = (P("mem", "lat", None, None), P(), P(), P(None, "lat", None), P(), P())
    out_specs = (P("mem", "lat", None, None), P(), P())
    return jax.shard_map(shards, mesh=mesh, in_specs=in_specs, out_specs=out_specs, check_vma=False)
```

profile of v0, /device:TPU:0, one launch (start us, length us, event | category | flops | bytes accessed | tf_op | source)
XLA Modules:
  0.0 686.2 jit_solution(3638382335253527599)
XLA Ops:
  7.2 2.2 fusion.275
  9.4 2.5 collective-permute-start
  13.2 3.5 fusion.177
  17.1 1.9 constant_dynamic-update-slice_fusion.3
  19.7 4.1 fusion.183
  23.7 4.0 fusion.173
  27.7 3.4 fusion.160
  31.1 3.4 fusion.163
  34.5 3.4 fusion.180
  38.0 3.4 fusion.168
  41.3 3.4 fusion.186
  44.7 21.2 %multiply_convert_fusion = (bf16[4,2,1440,128]{3,2,1,0:T(8,128)(2,1)}, f32[4,2,1440,128]{3,2,1,0:T(8,128)}) fusion(bf16[3,3,128,128]{3,2,1,0:T(8,128)(2,1)S(1)} %copy-done.21, bf16[4,4,1,128]{3,2,1,0:T(2,128)(2,1)S(1)} %get-tuple-element.58, bf16[4,4,1440,128]{3,2,1,0:T(8,128)(2,1)} %copy-done.2, f32[4,2,1440,128]{3,2,1,0:T(8,128)} %fusion.168, ...), kind=kOutput, calls=%fused_computation.41 | convolution fusion | flops 408453120 | bytes 61972480 | tf_op jit(solution)/shard_map/mrlc,co->mrlo/dot_general | solution.py:45
  66.0 2.2 fusion.274
  68.1 30.4 %collective-permute-start.2 = (bf16[4,1,1440,128]{3,2,1,0:T(8,128)(2,1)S(1)}, bf16[4,1,1440,128]{3,2,1,0:T(8,128)(2,1)S(1)}, u32[]{:S(2)}, u32[]{:S(2)}) collective-permute-start(bf16[4,1,1440,128]{3,2,1,0:T(8,128)(2,1)S(1)} %get-tuple-element.64), channel_id=1, source_target_pairs={{0,1},{1,2},{2,3},{3,4},{4,5},{5,6},{6,7},{8,9},{9,10},{10,11},{11... | collective-permute-start | bytes 4423688 | tf_op jit(solution)/shard_map/ppermute | solution.py:15
  100.0 1.8 fusion.218
  101.9 1.8 collective-permute-done.3
  103.7 7.3 %fusion.7 = (bf16[4,4,1441,128]{3,2,1,0:T(8,128)(2,1)S(1)}, bf16[4,4,1441,128]{3,2,1,0:T(8,128)(2,1)S(1)}) fusion(bf16[4,1,1440,128]{3,2,1,0:T(8,128)(2,1)S(1)} %collective-permute-done.3, bf16[4,2,1440,128]{3,2,1,0:T(8,128)(2,1)S(1)} %copy-done.5, bf16[4,1,1440,128]{3,2,1,0:T(8,128)(2,1)S(1)} %collective-permute-done.2), kind=kLoop, calls=%fused_computation.26 | loop fusion | flops 70828032 | bytes 17702912 | tf_op jit(solution)/shard_map/concatenate | solution.py:26
  111.0 4.1 fusion.76
  115.1 3.6 fusion.84
  118.7 3.6 fusion.92
  122.3 3.6 fusion.80
  126.0 3.6 fusion.88
  131.4 1.8 fusion.55
  133.2 8.2 %fusion.71 = bf16[4,69,2,1440]{3,1,2,0:T(8,128)(2,1)} fusion(bf16[4,4,1441,128]{3,2,1,0:T(8,128)(2,1)S(1)} %get-tuple-element.57, f32[4,2,1440,69]{2,3,1,0:T(8,128)S(1)} %fusion.53, f32[4,2,1440,69]{2,3,1,0:T(8,128)} %fusion.76, f32[4,2,1440,69]{2,3,1,0:T(8,128)} %fusion.80, f32[4,2,1440,69]{2,3,1,0:T(8,128)S(1)} %fusion.218, ...), kind=kOutput, calls=%fused_computation.109 | convolution fusion | flops 210643200 | bytes 32868864 | tf_op jit(solution)/shard_map/mrlc,cv->mvrl/dot_general | solution.py:59
  141.4 8.4 %copy.54 = bf16[4,69,2,1440]{1,2,0,3:T(2,128)(2,1)} copy(bf16[4,69,2,1440]{3,1,2,0:T(8,128)(2,1)} %fusion.71) | data formatting | bytes 3179520 | tf_op jit(solution)/shard_map/convert_element_type | solution.py:145
  149.8 4.9 all-to-all-start
  155.2 46.0 %all-to-all-done = bf16[4,69,2,1440]{1,2,0,3:T(2,128)(2,1)} async-done(((bf16[4,69,2,1440]{1,2,0,3:T(2,128)(2,1)}), bf16[4,69,2,1440]{1,2,0,3:T(2,128)(2,1)}, u32[]{:S(2)}, u32[]{:S(2)}) %all-to-all-start) | async-done | bytes 1589792 | tf_op jit(solution)/shard_map/all_to_all | solution.py:150
  201.1 7.7 %copy.55 = bf16[4,69,2,1440]{3,0,2,1:T(4,128)(2,1)S(1)} copy(bf16[4,69,2,1440]{1,2,0,3:T(2,128)(2,1)} %all-to-all-done) | data formatting | bytes 3179520 | tf_op jit(solution)/shard_map/all_to_all | solution.py:150
  208.9 3.8 reshape.78
  212.7 5.6 copy.57
  218.3 3.7 copy.60
  222.1 61.3 %while.10 = (s32[]{:T(128)}, f32[23,16,3,2,360]{4,1,3,2,0:T(8,128)}, f32[23,16,3,2,360]{4,3,2,0,1:T(2,128)}, f32[23,3]{1,0:T(8,128)S(1)}, s32[]{:T(128)}) while((s32[]{:T(128)}, f32[23,16,3,2,360]{4,1,3,2,0:T(8,128)}, f32[23,16,3,2,360]{4,3,2,0,1:T(2,128)}, f32[23,3]{1,0:T(8,128)S(1)}, s32[]{:T(128)}) %tuple.48), condition=%wide.region_2.3_spmd, body=%wide.region_0.2_spmd.sunk | while | flops 3283202 | bytes 1253493 | solution.py:159
  283.4 2.5 broadcast_multiply_fusion
  286.4 3.2 fusion.34
  291.0 25.7 %all_to_all.27 = bf16[16,69,2,360]{3,2,1,0:T(2,128)(2,1)S(1)} all-to-all(bf16[16,69,2,360]{3,2,1,0:T(2,128)(2,1)S(1)} %copy.62), channel_id=1, replica_groups=mesh['mem'=4,'lat'=8] {'mem'}, dimensions={0} | all-to-all | bytes 3179520 | tf_op jit(solution)/shard_map/all_to_all | solution.py:167
  316.9 2.6 copy.64
  319.5 3.5 all_to_all.24
  323.0 2.7 fusion.122
  334.7 22.2 %collective-permute-start.4 = (bf16[4,69,1,1440]{3,0,2,1:T(4,128)(2,1)S(1)}, bf16[4,69,1,1440]{3,0,2,1:T(4,128)(2,1)S(1)}, u32[]{:S(2)}, u32[]{:S(2)}) collective-permute-start(bf16[4,69,1,1440]{3,0,2,1:T(4,128)(2,1)S(1)} %copy.65), channel_id=1, source_target_pairs={{0,1},{1,2},{2,3},{3,4},{4,5},{5,6},{6,7},{8,9},{9,10},{10,11},{11... | collective-permute-start | bytes 2384648 | tf_op jit(solution)/shard_map/ppermute | solution.py:15
  360.5 3.5 fusion.216
  364.4 43.1 %collective-permute-done.5 = bf16[4,69,1,1440]{3,0,2,1:T(4,128)(2,1)S(1)} collective-permute-done((bf16[4,69,1,1440]{3,0,2,1:T(4,128)(2,1)S(1)}, bf16[4,69,1,1440]{3,0,2,1:T(4,128)(2,1)S(1)}, u32[]{:S(2)}, u32[]{:S(2)}) %collective-permute-start.5) | collective-permute-done | bytes 794912 | tf_op jit(solution)/shard_map/ppermute | solution.py:17
  407.8 4.2 fusion.98
  412.0 4.2 fusion.95
  416.3 4.1 fusion.104
  420.4 4.1 fusion.108
  424.5 4.2 fusion.101
  428.6 4.0 fusion.57
  432.6 3.6 fusion.61
  436.2 21.4 %fusion.19 = bf16[4,2,1440,128]{3,2,1,0:T(8,128)(2,1)} fusion(f32[4,2,1440,128]{3,2,1,0:T(8,128)} %get-tuple-element.82, f32[4,2,1440,128]{3,2,1,0:T(8,128)} %fusion.61, f32[4,2,1440,128]{3,2,1,0:T(8,128)} %fusion.108, f32[4,2,1440,128]{3,2,1,0:T(8,128)} %fusion.95, f32[4,2,1440,128]{3,2,1,0:T(8,128)} %fusion.216, f32[4,2,1440,128]{3,2,1,0:T(8,128)} %fusion.101, ...), kind=kOutput, calls=%fused_computation.39 | convolution fusion | flops 245007360 | bytes 59526144 | tf_op jit(solution)/shard_map/mvrl,cv->mrlc/dot_general | solution.py:73
  457.6 3.9 fusion.118
  463.4 2.8 fusion.111
  473.5 17.4 %collective-permute-start.6 = (bf16[4,1,1440,128]{3,2,1,0:T(8,128)(2,1)}, bf16[4,1,1440,128]{3,2,1,0:T(8,128)(2,1)}, u32[]{:S(2)}, u32[]{:S(2)}) collective-permute-start(bf16[4,1,1440,128]{3,2,1,0:T(8,128)(2,1)} %get-tuple-element.63), channel_id=1, source_target_pairs={{0,1},{1,2},{2,3},{3,4},{4,5},{5,6},{6,7},{8,9},{9,10},{10,11},{11... | collective-permute-start | bytes 4423688 | tf_op jit(solution)/shard_map/ppermute | solution.py:15
  493.8 5.2 fusion.175
  499.1 122.8 %all-reduce.3.cloned.1.call-done = (f32[3,3,128,128]{3,2,1,0:T(8,128)}, f32[3,3,128,69]{2,3,1,0:T(8,128)}) async-done(((f32[3,3,128,128]{3,2,1,0:T(8,128)}, f32[3,3,128,69]{2,3,1,0:T(8,128)}), (f32[3,3,128,128]{3,2,1,0:T(8,128)}, f32[3,3,128,69]{2,3,1,0:T(8,128)})) %all-reduce.3.cloned.1.call-update) | async-done | bytes 907792 | tf_op jit(solution)/shard_map/psum | solution.py:178
  623.6 1.9 broadcast_multiply_fusion.1
  625.5 7.7 %fusion.4 = (bf16[4,4,1441,128]{3,2,1,0:T(8,128)(2,1)S(1)}, bf16[4,4,1441,128]{3,2,1,0:T(8,128)(2,1)S(1)}) fusion(bf16[4,1,1440,128]{3,2,1,0:T(8,128)(2,1)S(1)} %collective-permute-done.7, bf16[4,2,1440,128]{3,2,1,0:T(8,128)(2,1)} %fusion.19, bf16[4,1,1440,128]{3,2,1,0:T(8,128)(2,1)} %collective-permute-done.6), kind=kLoop, calls=%fused_computation.17 | loop fusion | flops 70828032 | bytes 17702912 | tf_op jit(solution)/shard_map/concatenate | solution.py:26
  633.2 3.9 fusion.45
  637.5 3.5 fusion.49
  641.0 3.6 fusion.43
  644.6 3.5 fusion.47
  648.0 3.5 fusion.51
  651.5 4.8 fusion.24
  656.3 3.5 fusion.20
  659.8 19.4 %add_convert_fusion = bf16[4,2,1440,128]{3,2,1,0:T(8,128)(2,1)} fusion(f32[4,2,1440,128]{3,2,1,0:T(8,128)} %fusion.24, f32[4,2,1440,128]{3,2,1,0:T(8,128)} %fusion.43, f32[4,2,1440,128]{3,2,1,0:T(8,128)} %fusion.45, f32[4,2,1440,128]{3,2,1,0:T(8,128)} %fusion.175, f32[4,2,1440,128]{3,2,1,0:T(8,128)} %fusion.47, f32[4,2,1440,128]{3,2,1,0:T(8,128)} %fusion.49, ...), kind=kOutput, calls=%fused_computation.40 | convolution fusion | flops 390758400 | bytes 53116928 | tf_op jit(solution)/shard_map/mrlo,co->mrlc/dot_general | solution.py:92
  (237 shorter events, 96.4 us)
Async XLA Ops:
  7.2 147.7 %copy-start = (f32[69,2,1440]{2,1,0:T(2,128)S(1)}, f32[69,2,1440]{2,1,0:T(2,128)}, u32[]{:S(2)}) copy-start(f32[69,2,1440]{2,1,0:T(2,128)} %param.11) | copy-start | bytes 2384644
  7.2 6.0 copy-start.9
  7.2 6.0 copy-start.21
  9.4 7.3 %collective-permute-start = (bf16[4,1,1440,128]{3,2,1,0:T(8,128)(2,1)S(1)}, bf16[4,1,1440,128]{3,2,1,0:T(8,128)(2,1)S(1)}, u32[]{:S(2)}, u32[]{:S(2)}) collective-permute-start(bf16[4,1,1440,128]{3,2,1,0:T(8,128)(2,1)S(1)} %get-tuple-element.69), channel_id=1, source_target_pairs={{0,1},{1,2},{2,3},{3,4},{4,5},{5,6},{6,7},{8,9},{9,10},{10,11},{11... | collective-permute-start | bytes 4423688 | tf_op jit(solution)/shard_map/ppermute | solution.py:15
  11.9 7.2 %collective-permute-start.1 = (bf16[4,1,1440,128]{3,2,1,0:T(8,128)(2,1)S(1)}, bf16[4,1,1440,128]{3,2,1,0:T(8,128)(2,1)S(1)}, u32[]{:S(2)}, u32[]{:S(2)}) collective-permute-start(bf16[4,1,1440,128]{3,2,1,0:T(8,128)(2,1)S(1)} %get-tuple-element.70), channel_id=1, source_target_pairs={{1,0},{2,1},{3,2},{4,3},{5,4},{6,5},{7,6},{9,8},{10,9},{11,10},{12... | collective-permute-start | bytes 4423688 | tf_op jit(solution)/shard_map/ppermute | solution.py:17
  19.0 22.4 %copy-start.15 = (bf16[4,3,1440,128]{3,2,1,0:T(8,128)(2,1)}, bf16[4,3,1440,128]{3,2,1,0:T(8,128)(2,1)S(1)}, u32[]{:S(2)}) copy-start(bf16[4,3,1440,128]{3,2,1,0:T(8,128)(2,1)S(1)} %get-tuple-element.66) | copy-start | bytes 13271044
  19.6 14.9 %copy-start.2 = (bf16[4,4,1440,128]{3,2,1,0:T(8,128)(2,1)}, bf16[4,4,1440,128]{3,2,1,0:T(8,128)(2,1)S(1)}, u32[]{:S(2)}) copy-start(bf16[4,4,1440,128]{3,2,1,0:T(8,128)(2,1)S(1)} %get-tuple-element.75) | copy-start | bytes 17694724
  19.6 18.3 %copy-start.13 = (bf16[4,3,1440,128]{3,2,1,0:T(8,128)(2,1)}, bf16[4,3,1440,128]{3,2,1,0:T(8,128)(2,1)S(1)}, u32[]{:S(2)}) copy-start(bf16[4,3,1440,128]{3,2,1,0:T(8,128)(2,1)S(1)} %get-tuple-element.76) | copy-start | bytes 13271044
  66.0 34.1 %copy-start.5 = (bf16[4,2,1440,128]{3,2,1,0:T(8,128)(2,1)S(1)}, bf16[4,2,1440,128]{3,2,1,0:T(8,128)(2,1)}, u32[]{:S(2)}) copy-start(bf16[4,2,1440,128]{3,2,1,0:T(8,128)(2,1)} %get-tuple-element.81) | copy-start | bytes 8847364
  66.0 34.1 %copy-start.22 = (bf16[3,3,128,69]{2,3,1,0:T(8,128)(2,1)S(1)}, bf16[3,3,128,69]{2,3,1,0:T(8,128)(2,1)}, u32[]{:S(2)}) copy-start(bf16[3,3,128,69]{2,3,1,0:T(8,128)(2,1)} %param.10) | copy-start | bytes 476932
  68.1 33.7 %collective-permute-start.2 = (bf16[4,1,1440,128]{3,2,1,0:T(8,128)(2,1)S(1)}, bf16[4,1,1440,128]{3,2,1,0:T(8,128)(2,1)S(1)}, u32[]{:S(2)}, u32[]{:S(2)}) collective-permute-start(bf16[4,1,1440,128]{3,2,1,0:T(8,128)(2,1)S(1)} %get-tuple-element.64), channel_id=1, source_target_pairs={{0,1},{1,2},{2,3},{3,4},{4,5},{5,6},{6,7},{8,9},{9,10},{10,11},{11... | collective-permute-start | bytes 4423688 | tf_op jit(solution)/shard_map/ppermute | solution.py:15
  98.5 5.2 collective-permute-start.3
  101.9 29.5 %copy-start.19 = (bf16[4,1,1440,128]{3,2,1,0:T(8,128)(2,1)}, bf16[4,1,1440,128]{3,2,1,0:T(8,128)(2,1)S(1)}, u32[]{:S(2)}) copy-start(bf16[4,1,1440,128]{3,2,1,0:T(8,128)(2,1)S(1)} %collective-permute-done.2) | copy-start | bytes 4423684
  103.7 25.8 %copy-start.17 = (bf16[4,1,1440,128]{3,2,1,0:T(8,128)(2,1)}, bf16[4,1,1440,128]{3,2,1,0:T(8,128)(2,1)S(1)}, u32[]{:S(2)}) copy-start(bf16[4,1,1440,128]{3,2,1,0:T(8,128)(2,1)S(1)} %collective-permute-done.3) | copy-start | bytes 4423684
  111.0 7.7 %copy-start.12 = (bf16[4,4,1441,128]{3,2,1,0:T(8,128)(2,1)}, bf16[4,4,1441,128]{3,2,1,0:T(8,128)(2,1)S(1)}, u32[]{:S(2)}) copy-start(bf16[4,4,1441,128]{3,2,1,0:T(8,128)(2,1)S(1)} %get-tuple-element.56) | copy-start | bytes 17707012
  111.0 22.2 %copy-start.11 = (bf16[4,4,1441,128]{3,2,1,0:T(8,128)(2,1)}, bf16[4,4,1441,128]{3,2,1,0:T(8,128)(2,1)S(1)}, u32[]{:S(2)}) copy-start(bf16[4,4,1441,128]{3,2,1,0:T(8,128)(2,1)S(1)} %get-tuple-element.57) | copy-start | bytes 17707012
  141.4 13.4 %copy-start.26 = (f32[69]{0:T(128)S(1)}, f32[69]{0:T(128)}, u32[]{:S(2)}) copy-start(f32[69]{0:T(128)} %param.13) | copy-start | bytes 832
  141.4 13.4 %copy-start.27 = (f32[69]{0:T(128)S(1)}, f32[69]{0:T(128)}, u32[]{:S(2)}) copy-start(f32[69]{0:T(128)} %param.12) | copy-start | bytes 832
  149.8 51.3 %all-to-all-start = ((bf16[4,69,2,1440]{1,2,0,3:T(2,128)(2,1)}), bf16[4,69,2,1440]{1,2,0,3:T(2,128)(2,1)}, u32[]{:S(2)}, u32[]{:S(2)}) async-start(bf16[4,69,2,1440]{1,2,0,3:T(2,128)(2,1)} %copy.54), calls=%async_computation | async-start | bytes 5898240 | tf_op jit(solution)/shard_map/all_to_all | solution.py:150
  154.7 467.1 %all-reduce.3.cloned.1.call-start = ((), (), s32[]{:S(2)}) async-start(), calls=%async_computation.2 | async-start | bytes 1843200 | tf_op jit(solution)/shard_map/psum | solution.py:178
  212.7 5.6 copy-start.14
  283.4 3.0 copy-start.16
  323.0 2.9 copy-start.6
  323.0 3.1 copy-start.20
  325.7 2.3 slice-start.2
  326.1 2.3 slice-start.3
  326.1 3.7 slice-start.4
  328.4 1.9 slice-start.5
  333.1 25.3 %copy-start.18 = (bf16[4,1,1440,128]{3,2,1,0:T(8,128)(2,1)S(1)}, bf16[4,1,1440,128]{3,2,1,0:T(8,128)(2,1)}, u32[]{:S(2)}) copy-start(bf16[4,1,1440,128]{3,2,1,0:T(8,128)(2,1)} %copy-done.17) | copy-start | bytes 4423684
  334.7 29.3 %collective-permute-start.4 = (bf16[4,69,1,1440]{3,0,2,1:T(4,128)(2,1)S(1)}, bf16[4,69,1,1440]{3,0,2,1:T(4,128)(2,1)S(1)}, u32[]{:S(2)}, u32[]{:S(2)}) collective-permute-start(bf16[4,69,1,1440]{3,0,2,1:T(4,128)(2,1)S(1)} %copy.65), channel_id=1, source_target_pairs={{0,1},{1,2},{2,3},{3,4},{4,5},{5,6},{6,7},{8,9},{9,10},{10,11},{11... | collective-permute-start | bytes 2384648 | tf_op jit(solution)/shard_map/ppermute | solution.py:15
  356.9 50.5 %collective-permute-start.5 = (bf16[4,69,1,1440]{3,0,2,1:T(4,128)(2,1)S(1)}, bf16[4,69,1,1440]{3,0,2,1:T(4,128)(2,1)S(1)}, u32[]{:S(2)}, u32[]{:S(2)}) collective-permute-start(bf16[4,69,1,1440]{3,0,2,1:T(4,128)(2,1)S(1)} %copy.66), channel_id=1, source_target_pairs={{1,0},{2,1},{3,2},{4,3},{5,4},{6,5},{7,6},{9,8},{10,9},{11,10},{12... | collective-permute-start | bytes 2384648 | tf_op jit(solution)/shard_map/ppermute | solution.py:17
  359.1 1.4 copy-start.23
  360.5 3.7 copy-start.25
  407.6 16.8 %copy-start.7 = (bf16[4,69,4,1440]{3,1,2,0:T(8,128)(2,1)}, bf16[4,69,4,1440]{3,1,2,0:T(8,128)(2,1)S(1)}, u32[]{:S(2)}) copy-start(bf16[4,69,4,1440]{3,1,2,0:T(8,128)(2,1)S(1)} %get-tuple-element.78) | copy-start | bytes 9538564
  457.6 4.0 copy-start.3
  457.6 8.6 %slice-start = ((s8[5898240]{0:T(1024)(128)(4,1)}), s8[4194304]{0:T(1024)(128)(4,1)S(1)}, s32[]{:S(2)}) async-start(s8[5898240]{0:T(1024)(128)(4,1)} %bitcast.371), calls=%async_computation.3 | async-start | bytes 8388608
  461.6 4.6 slice-start.1
  467.2 1.8 copy-start.10
  469.1 21.9 %slice-start.6 = ((s8[4423680]{0:T(1024)(128)(4,1)}), s8[4194304]{0:T(1024)(128)(4,1)S(1)}, s32[]{:S(2)}) async-start(s8[4423680]{0:T(1024)(128)(4,1)} %bitcast.377), calls=%async_computation.9 | async-start | bytes 8388608
  470.1 20.8 %slice-start.7 = ((s8[4423680]{0:T(1024)(128)(4,1)}), s8[229376]{0:T(1024)(128)(4,1)S(1)}, s32[]{:S(2)}) async-start(s8[4423680]{0:T(1024)(128)(4,1)} %bitcast.377), calls=%async_computation.10 | async-start | bytes 458752
  472.2 153.3 %collective-permute-start.7 = (bf16[4,1,1440,128]{3,2,1,0:T(8,128)(2,1)}, bf16[4,1,1440,128]{3,2,1,0:T(8,128)(2,1)S(1)}, u32[]{:S(2)}, u32[]{:S(2)}) collective-permute-start(bf16[4,1,1440,128]{3,2,1,0:T(8,128)(2,1)} %get-tuple-element.62), channel_id=1, source_target_pairs={{1,0},{2,1},{3,2},{4,3},{5,4},{6,5},{7,6},{9,8},{10,9},{11,10},{12... | collective-permute-start | bytes 4423688 | tf_op jit(solution)/shard_map/ppermute | solution.py:17
  473.5 152.0 %collective-permute-start.6 = (bf16[4,1,1440,128]{3,2,1,0:T(8,128)(2,1)}, bf16[4,1,1440,128]{3,2,1,0:T(8,128)(2,1)}, u32[]{:S(2)}, u32[]{:S(2)}) collective-permute-start(bf16[4,1,1440,128]{3,2,1,0:T(8,128)(2,1)} %get-tuple-element.63), channel_id=1, source_target_pairs={{0,1},{1,2},{2,3},{3,4},{4,5},{5,6},{6,7},{8,9},{9,10},{10,11},{11... | collective-permute-start | bytes 4423688 | tf_op jit(solution)/shard_map/ppermute | solution.py:15
  493.0 0.8 copy-start.24
  633.2 4.3 copy-start.8
  648.0 3.5 copy-start.4
  659.8 19.4 %copy-start.1 = (f32[69,2,1440]{2,1,0:T(2,128)S(1)}, f32[69,2,1440]{2,1,0:T(2,128)}, u32[]{:S(2)}) copy-start(f32[69,2,1440]{2,1,0:T(2,128)} %param.11) | copy-start | bytes 2384644
Sparse Core Ops, SparseCore 0:
  494.0 127.8 all-reduce.2
where the time goes:
time: 697 us; the launch traced here: 686 us
  waiting for transfers between devices  214 us (31%)
  matrix products  210 us (30%)
  local copies, waits for them, and re-layouts  90.5 us (13%)
  starting transfers between devices  82.9 us (12%)
  other arithmetic  47.9 us (7%)
  blocking collectives  25.7 us (4%)
  between operations  14.9 us (2%)
    psum x1, waiting for transfers between devices, shards(): inner_sum, head_sum = lax.psum((inner_grad, head_grad), ('mem', 'lat'))  123 us
    ppermute x4, starting transfers between devices, padded_2(): lax.ppermute(tail, axis, [(i, (i + 1) % count) for i in range(ends)])  72.5 us
    dot_general x9, matrix products, field_back(): jnp.einsum('mvrl,cv->mrlc', padded_grad[:, :, 2 - row_off:2 - row_off + b...  53.3 us
    dot_general x9, matrix products, hidden_back(): jnp.einsum('mrlo,co->mrlc', padded_grad[:, 2 - row_off:2 - row_off + band...  50.8 us
    dot_general x9, matrix products, hidden_conv(): jnp.einsum('mrlc,co->mrlo', padded[:, row_off:row_off + band_rows, col_of...  49.8 us
    all_to_all x1, waiting for transfers between devices, shards(): lax.all_to_all(field, 'mem', split_axis=3, concat_axis=0, tiled=True)  46 us
    ppermute x4, waiting for transfers between devices, padded_2(): lax.ppermute(head, axis, [((i + 1) % count, i) for i in range(ends)])  44.9 us
    dot_general x9, matrix products, field_conv(): jnp.einsum('mrlc,cv->mvrl', padded[:, row_off:row_off + band_rows, col_of...  32.1 us
  transfers between devices with their start and end apart: 10, of which 4 were waited for; matrix products, arithmetic and copies ran while one was open for 4% of the time, Pallas kernels for 0%

commit v1 on v0

--- a/solution.py
+++ b/solution.py
@@ -2,6 +2,17 @@
 import jax.numpy as jnp
 from jax import lax
 from jax.sharding import PartitionSpec as P
+
+
+def split_up(value, dim, size):
+    before, after = (value.shape[:dim], value.shape[dim + 1 :])
+    return jnp.moveaxis(value.reshape(*before, size, -1, *after), dim, 0)
+
+
+def laid_out(blocks, dim):
+    shape = list(blocks.shape[1:])
+    shape[dim] *= blocks.shape[0]
+    return jnp.moveaxis(blocks, 0, dim).reshape(shape)
 
 
 def padded_2(cells, sides, width):
@@ -147,7 +158,14 @@
     group = 3
     blocks = variables // group
     inverse_blocks = inverse.reshape(blocks, group)
-    gathered = lax.all_to_all(field, "mem", split_axis=3, concat_axis=0, tiled=True)
+    size, index = (lax.axis_size("mem"), lax.axis_index("mem"))
+    blocks_2 = split_up(field, 3, size)
+    outs = [blocks_2[index]]
+    for step in range(1, size):
+        sent = blocks_2[(index + step) % size]
+        outs.append(lax.ppermute(sent, "mem", [(i_2, (i_2 + step) % size) for i_2 in range(size)]))
+    blocks_2 = jnp.stack(outs)[(index - jnp.arange(size)) % size]
+    gathered = laid_out(blocks_2, 0)
     values = gathered.astype(jnp.float32)
     members = values.shape[0]
     piece_cells = values.shape[3]

time: 697 us -> 665 us (0.954)
  waiting for transfers between devices: 214 us -> 167 us
  local copies, waits for them, and re-layouts: 90.5 us -> 76.6 us
  starting transfers between devices: 82.9 us -> 91.3 us
  matrix products: 210 us -> 218 us
  other arithmetic: 47.9 us -> 55.1 us
    all_to_all x1 -> x0, waiting for transfers between devices: 46 us -> none  [shards(): lax.all_to_all(field, 'mem', split_axis=3, concat_axis=0, tiled=True)]
    ppermute x4, waiting for transfers between devices: 44.9 us -> 31.5 us  [padded_2(): lax.ppermute(head, axis, [((i + 1) % count, i) for i in range(ends)])]
    ppermute x0 -> x3, waiting for transfers between devices: none -> 13.2 us  [shards(): lax.ppermute(sent, 'mem', [(i_2, (i_2 + step) % size) for i_2 in range(si...]
    transpose x3 -> x1, local copies, waits for them, and re-layouts: 13.2 us -> 3.07 us  [split_groups(): return jnp.moveaxis(shaped, 1, 0)]
    convert_element_type x1 -> x0, local copies, waits for them, and re-layouts: 8.43 us -> none  [shards(): field = field_conv(hidden_wrap, conv_head, band_rows).astype(jnp.bfloat16)]
    all_to_all x1 -> x0, local copies, waits for them, and re-layouts: 7.72 us -> none  [shards(): lax.all_to_all(field, 'mem', split_axis=3, concat_axis=0, tiled=True)]
    ppermute x4, starting transfers between devices: 72.5 us -> 80.2 us  [padded_2(): lax.ppermute(tail, axis, [(i, (i + 1) % count) for i in range(ends)])]
  transfers between devices with their start and end apart: 10 -> 12, of which waited for: 4 -> 6; matrix products, arithmetic and copies ran while one was open for 4% -> 4% of each run, Pallas kernels for 0% -> 0%
where the time goes in v1:
time: 665 us; the launch traced here: 654 us
  matrix products  218 us (33%)
  waiting for transfers between devices  167 us (25%)
  starting transfers between devices  91.3 us (14%)
  local copies, waits for them, and re-layouts  76.6 us (12%)
  other arithmetic  55.1 us (8%)
  blocking collectives  30.5 us (5%)
  between operations  15.2 us (2%)
    psum x1, waiting for transfers between devices, shards(): inner_sum, head_sum = lax.psum((inner_grad, head_grad), ('mem', 'lat'))  123 us
    ppermute x4, starting transfers between devices, padded_2(): lax.ppermute(tail, axis, [(i, (i + 1) % count) for i in range(ends)])  80.2 us
    dot_general x9, matrix products, field_back(): jnp.einsum('mvrl,cv->mrlc', padded_grad[:, :, 2 - row_off:2 - row_off + b...  53.1 us
    dot_general x9, matrix products, hidden_back(): jnp.einsum('mrlo,co->mrlc', padded_grad[:, 2 - row_off:2 - row_off + band...  50.8 us
    dot_general x9, matrix products, hidden_conv(): jnp.einsum('mrlc,co->mrlo', padded[:, row_off:row_off + band_rows, col_of...  49.8 us
    dot_general x9, matrix products, field_conv(): jnp.einsum('mrlc,cv->mvrl', padded[:, row_off:row_off + band_rows, col_of...  37.3 us
    ppermute x4, waiting for transfers between devices, padded_2(): lax.ppermute(head, axis, [((i + 1) % count, i) for i in range(ends)])  31.5 us
    all_to_all x1, blocking collectives, shards(): lax.all_to_all(gradient, 'mem', split_axis=0, concat_axis=3, tiled=True)  30.5 us
  transfers between devices with their start and end apart: 12, of which 6 were waited for; matrix products, arithmetic and copies ran while one was open for 4% of the time, Pallas kernels for 0%

profile of v1, /device:TPU:0, one launch (start us, length us, event | category | flops | bytes accessed | tf_op | source)
XLA Modules:
  0.0 654.5 jit_solution(16913464918550817654)
XLA Ops:
  7.2 2.2 fusion.277
  9.4 2.5 collective-permute-start
  13.2 3.5 fusion.177
  19.7 4.1 fusion.183
  23.8 4.0 fusion.173
  27.8 3.4 fusion.160
  31.2 3.4 fusion.163
  34.6 3.4 fusion.180
  38.0 3.4 fusion.168
  41.4 3.4 fusion.186
  44.8 21.2 %multiply_convert_fusion = (bf16[4,2,1440,128]{3,2,1,0:T(8,128)(2,1)}, f32[4,2,1440,128]{3,2,1,0:T(8,128)}) fusion(bf16[3,3,128,128]{3,2,1,0:T(8,128)(2,1)S(1)} %copy-done.16, bf16[4,4,1,128]{3,2,1,0:T(2,128)(2,1)S(1)} %get-tuple-element.54, bf16[4,4,1440,128]{3,2,1,0:T(8,128)(2,1)} %copy-done.2, f32[4,2,1440,128]{3,2,1,0:T(8,128)} %fusion.168, ...), kind=kOutput, calls=%fused_computation.42 | convolution fusion | flops 408453120 | bytes 61972480 | tf_op jit(solution)/shard_map/mrlc,co->mrlo/dot_general | solution.py:56
  66.1 3.7 fusion.276
  69.8 31.7 %collective-permute-start.2 = (bf16[4,1,1440,128]{3,2,1,0:T(8,128)(2,1)}, bf16[4,1,1440,128]{3,2,1,0:T(8,128)(2,1)}, u32[]{:S(2)}, u32[]{:S(2)}) collective-permute-start(bf16[4,1,1440,128]{3,2,1,0:T(8,128)(2,1)} %get-tuple-element.60), channel_id=1, source_target_pairs={{0,1},{1,2},{2,3},{3,4},{4,5},{5,6},{6,7},{8,9},{9,10},{10,11},{11... | collective-permute-start | bytes 4423688 | tf_op jit(solution)/shard_map/ppermute | solution.py:26
  102.9 3.8 fusion.218
  107.1 9.6 %fusion.7 = (bf16[4,4,1441,128]{3,2,1,0:T(8,128)(2,1)S(1)}, bf16[4,4,1441,128]{3,2,1,0:T(8,128)(2,1)S(1)}) fusion(bf16[4,1,1440,128]{3,2,1,0:T(8,128)(2,1)} %collective-permute-done.3, bf16[4,2,1440,128]{3,2,1,0:T(8,128)(2,1)S(1)} %copy-done.5, bf16[4,1,1440,128]{3,2,1,0:T(8,128)(2,1)} %collective-permute-done.2), kind=kLoop, calls=%fused_computation.27 | loop fusion | flops 70828032 | bytes 17702912 | tf_op jit(solution)/shard_map/concatenate | solution.py:37
  116.7 4.1 fusion.76
  120.7 3.7 fusion.84
  124.4 3.6 fusion.92
  128.0 3.6 fusion.80
  131.7 3.6 fusion.88
  135.2 3.2 fusion.53
  138.4 3.2 fusion.55
  141.6 8.5 %fusion.71 = bf16[4,69,2,1440]{3,1,2,0:T(8,128)(2,1)} fusion(bf16[4,4,1441,128]{3,2,1,0:T(8,128)(2,1)S(1)} %get-tuple-element.53, f32[4,2,1440,69]{2,3,1,0:T(8,128)S(1)} %fusion.53, f32[4,2,1440,69]{2,3,1,0:T(8,128)} %fusion.76, f32[4,2,1440,69]{2,3,1,0:T(8,128)} %fusion.80, f32[4,2,1440,69]{2,3,1,0:T(8,128)S(1)} %fusion.218, ...), kind=kOutput, calls=%fused_computation.110 | convolution fusion | flops 210643200 | bytes 31071744 | tf_op jit(solution)/shard_map/mrlc,cv->mvrl/dot_general | solution.py:70
  150.1 4.2 reshape.91
  154.4 3.6 constant_dynamic-slice_fusion.5
  160.5 2.6 collective-permute-start.5
  165.6 3.8 collective-permute-done.4
  169.4 9.4 %collective-permute-done.5 = bf16[4,69,2,360]{3,1,2,0:T(8,128)(2,1)} collective-permute-done((bf16[4,69,2,360]{3,1,2,0:T(8,128)(2,1)S(1)}, bf16[4,69,2,360]{3,1,2,0:T(8,128)(2,1)}, u32[]{:S(2)}, u32[]{:S(2)}) %collective-permute-start.5) | collective-permute-done | bytes 397472 | tf_op jit(solution)/shard_map/ppermute | solution.py:166
  178.9 2.9 pad_maximum_fusion.22
  181.7 2.4 gather_fusion
  184.2 3.1 copy.33
  189.3 61.3 %while.10 = (s32[]{:T(128)}, f32[23,16,3,2,360]{4,1,3,2,0:T(8,128)}, f32[23,16,3,2,360]{4,3,2,0,1:T(2,128)}, f32[23,3]{1,0:T(8,128)S(1)}, s32[]{:T(128)}) while((s32[]{:T(128)}, f32[23,16,3,2,360]{4,1,3,2,0:T(8,128)}, f32[23,16,3,2,360]{4,3,2,0,1:T(2,128)}, f32[23,3]{1,0:T(8,128)S(1)}, s32[]{:T(128)}) %tuple.50), condition=%wide.region_2.3_spmd, body=%wide.region_0.2_spmd.sunk | while | flops 3283202 | bytes 1253493 | solution.py:177
  250.6 2.5 broadcast_multiply_fusion
  253.6 3.2 fusion.34
  258.2 30.5 %all_to_all.18 = bf16[16,69,2,360]{3,2,1,0:T(2,128)(2,1)S(1)} all-to-all(bf16[16,69,2,360]{3,2,1,0:T(2,128)(2,1)S(1)} %copy.37), channel_id=1, replica_groups=mesh['mem'=4,'lat'=8] {'mem'}, dimensions={0} | all-to-all | bytes 3179520 | tf_op jit(solution)/shard_map/all_to_all | solution.py:185
  288.9 2.6 copy.39
  291.5 3.5 all_to_all.16
  295.0 2.7 fusion.122
  297.9 2.2 fusion.156
  307.2 28.5 %collective-permute-start.7 = (bf16[4,69,1,1440]{3,0,2,1:T(4,128)(2,1)S(1)}, bf16[4,69,1,1440]{3,0,2,1:T(4,128)(2,1)S(1)}, u32[]{:S(2)}, u32[]{:S(2)}) collective-permute-start(bf16[4,69,1,1440]{3,0,2,1:T(4,128)(2,1)S(1)} %copy.40), channel_id=1, source_target_pairs={{0,1},{1,2},{2,3},{3,4},{4,5},{5,6},{6,7},{8,9},{9,10},{10,11},{11... | collective-permute-start | bytes 2384648 | tf_op jit(solution)/shard_map/ppermute | solution.py:26
  340.8 3.5 fusion.216
  344.7 31.0 %collective-permute-done.8 = bf16[4,69,1,1440]{3,0,2,1:T(4,128)(2,1)S(1)} collective-permute-done((bf16[4,69,1,1440]{3,0,2,1:T(4,128)(2,1)S(1)}, bf16[4,69,1,1440]{3,0,2,1:T(4,128)(2,1)S(1)}, u32[]{:S(2)}, u32[]{:S(2)}) %collective-permute-start.8) | collective-permute-done | bytes 794912 | tf_op jit(solution)/shard_map/ppermute | solution.py:28
  376.1 4.2 fusion.98
  380.4 4.3 fusion.95
  384.6 4.1 fusion.104
  388.7 4.1 fusion.108
  392.8 4.2 fusion.101
  397.0 3.7 fusion.57
  400.7 3.6 fusion.61
  404.3 21.4 %fusion.19 = bf16[4,2,1440,128]{3,2,1,0:T(8,128)(2,1)} fusion(f32[4,2,1440,128]{3,2,1,0:T(8,128)} %get-tuple-element.82, f32[4,2,1440,128]{3,2,1,0:T(8,128)} %fusion.61, f32[4,2,1440,128]{3,2,1,0:T(8,128)} %fusion.108, f32[4,2,1440,128]{3,2,1,0:T(8,128)} %fusion.95, f32[4,2,1440,128]{3,2,1,0:T(8,128)} %fusion.216, f32[4,2,1440,128]{3,2,1,0:T(8,128)} %fusion.101, ...), kind=kOutput, calls=%fused_computation.40 | convolution fusion | flops 245007360 | bytes 59526144 | tf_op jit(solution)/shard_map/mvrl,cv->mrlc/dot_general | solution.py:84
  425.7 3.9 fusion.118
  431.4 2.8 fusion.111
  441.6 17.5 %collective-permute-start.9 = (bf16[4,1,1440,128]{3,2,1,0:T(8,128)(2,1)}, bf16[4,1,1440,128]{3,2,1,0:T(8,128)(2,1)}, u32[]{:S(2)}, u32[]{:S(2)}) collective-permute-start(bf16[4,1,1440,128]{3,2,1,0:T(8,128)(2,1)} %get-tuple-element.59), channel_id=1, source_target_pairs={{0,1},{1,2},{2,3},{3,4},{4,5},{5,6},{6,7},{8,9},{9,10},{10,11},{11... | collective-permute-start | bytes 4423688 | tf_op jit(solution)/shard_map/ppermute | solution.py:26
  462.0 5.2 fusion.175
  467.2 122.7 %all-reduce.3.cloned.1.call-done = (f32[3,3,128,128]{3,2,1,0:T(8,128)}, f32[3,3,128,69]{2,3,1,0:T(8,128)}) async-done(((f32[3,3,128,128]{3,2,1,0:T(8,128)}, f32[3,3,128,69]{2,3,1,0:T(8,128)}), (f32[3,3,128,128]{3,2,1,0:T(8,128)}, f32[3,3,128,69]{2,3,1,0:T(8,128)})) %all-reduce.3.cloned.1.call-update) | async-done | bytes 907792 | tf_op jit(solution)/shard_map/psum | solution.py:196
  593.6 7.7 %fusion.4 = (bf16[4,4,1441,128]{3,2,1,0:T(8,128)(2,1)S(1)}, bf16[4,4,1441,128]{3,2,1,0:T(8,128)(2,1)S(1)}) fusion(bf16[4,1,1440,128]{3,2,1,0:T(8,128)(2,1)S(1)} %collective-permute-done.10, bf16[4,2,1440,128]{3,2,1,0:T(8,128)(2,1)} %fusion.19, bf16[4,1,1440,128]{3,2,1,0:T(8,128)(2,1)} %collective-permute-done.9), kind=kLoop, calls=%fused_computation.18 | loop fusion | flops 70828032 | bytes 17702912 | tf_op jit(solution)/shard_map/concatenate | solution.py:37
  601.3 3.9 fusion.45
  605.6 3.5 fusion.49
  609.1 3.6 fusion.43
  612.7 3.5 fusion.47
  616.1 3.5 fusion.51
  619.6 4.8 fusion.24
  624.4 3.5 fusion.20
  627.9 19.4 %add_convert_fusion = bf16[4,2,1440,128]{3,2,1,0:T(8,128)(2,1)} fusion(f32[4,2,1440,128]{3,2,1,0:T(8,128)} %fusion.24, f32[4,2,1440,128]{3,2,1,0:T(8,128)} %fusion.43, f32[4,2,1440,128]{3,2,1,0:T(8,128)} %fusion.45, f32[4,2,1440,128]{3,2,1,0:T(8,128)} %fusion.175, f32[4,2,1440,128]{3,2,1,0:T(8,128)} %fusion.47, f32[4,2,1440,128]{3,2,1,0:T(8,128)} %fusion.49, ...), kind=kOutput, calls=%fused_computation.41 | convolution fusion | flops 390758400 | bytes 53116928 | tf_op jit(solution)/shard_map/mrlo,co->mrlc/dot_general | solution.py:103
  (242 shorter events, 105.1 us)
Async XLA Ops:
  7.2 157.4 %copy-start = (f32[69,2,1440]{2,1,0:T(2,128)S(1)}, f32[69,2,1440]{2,1,0:T(2,128)}, u32[]{:S(2)}) copy-start(f32[69,2,1440]{2,1,0:T(2,128)} %param.11) | copy-start | bytes 2384644
  7.2 6.0 copy-start.16
  7.2 582.8 %all-reduce.3.cloned.1.call-start = ((), (), s32[]{:S(2)}) async-start(), calls=%async_computation.1 | async-start | bytes 1843200 | tf_op jit(solution)/shard_map/psum | solution.py:196
  7.2 6.0 copy-start.9
  9.4 7.3 %collective-permute-start = (bf16[4,1,1440,128]{3,2,1,0:T(8,128)(2,1)S(1)}, bf16[4,1,1440,128]{3,2,1,0:T(8,128)(2,1)S(1)}, u32[]{:S(2)}, u32[]{:S(2)}) collective-permute-start(bf16[4,1,1440,128]{3,2,1,0:T(8,128)(2,1)S(1)} %get-tuple-element.65), channel_id=1, source_target_pairs={{0,1},{1,2},{2,3},{3,4},{4,5},{5,6},{6,7},{8,9},{9,10},{10,11},{11... | collective-permute-start | bytes 4423688 | tf_op jit(solution)/shard_map/ppermute | solution.py:26
  11.9 7.2 %collective-permute-start.1 = (bf16[4,1,1440,128]{3,2,1,0:T(8,128)(2,1)S(1)}, bf16[4,1,1440,128]{3,2,1,0:T(8,128)(2,1)S(1)}, u32[]{:S(2)}, u32[]{:S(2)}) collective-permute-start(bf16[4,1,1440,128]{3,2,1,0:T(8,128)(2,1)S(1)} %get-tuple-element.66), channel_id=1, source_target_pairs={{1,0},{2,1},{3,2},{4,3},{5,4},{6,5},{7,6},{9,8},{10,9},{11,10},{12... | collective-permute-start | bytes 4423688 | tf_op jit(solution)/shard_map/ppermute | solution.py:28
  19.0 22.4 %copy-start.14 = (bf16[4,3,1440,128]{3,2,1,0:T(8,128)(2,1)}, bf16[4,3,1440,128]{3,2,1,0:T(8,128)(2,1)S(1)}, u32[]{:S(2)}) copy-start(bf16[4,3,1440,128]{3,2,1,0:T(8,128)(2,1)S(1)} %get-tuple-element.62) | copy-start | bytes 13271044
  19.7 15.0 %copy-start.2 = (bf16[4,4,1440,128]{3,2,1,0:T(8,128)(2,1)}, bf16[4,4,1440,128]{3,2,1,0:T(8,128)(2,1)S(1)}, u32[]{:S(2)}) copy-start(bf16[4,4,1440,128]{3,2,1,0:T(8,128)(2,1)S(1)} %get-tuple-element.75) | copy-start | bytes 17694724
  19.7 18.4 %copy-start.13 = (bf16[4,3,1440,128]{3,2,1,0:T(8,128)(2,1)}, bf16[4,3,1440,128]{3,2,1,0:T(8,128)(2,1)S(1)}, u32[]{:S(2)}) copy-start(bf16[4,3,1440,128]{3,2,1,0:T(8,128)(2,1)S(1)} %get-tuple-element.76) | copy-start | bytes 13271044
  66.1 36.8 %copy-start.19 = (bf16[3,3,128,69]{2,3,1,0:T(8,128)(2,1)S(1)}, bf16[3,3,128,69]{2,3,1,0:T(8,128)(2,1)}, u32[]{:S(2)}) copy-start(bf16[3,3,128,69]{2,3,1,0:T(8,128)(2,1)} %param.10) | copy-start | bytes 476932
  69.8 36.9 %collective-permute-start.2 = (bf16[4,1,1440,128]{3,2,1,0:T(8,128)(2,1)}, bf16[4,1,1440,128]{3,2,1,0:T(8,128)(2,1)}, u32[]{:S(2)}, u32[]{:S(2)}) collective-permute-start(bf16[4,1,1440,128]{3,2,1,0:T(8,128)(2,1)} %get-tuple-element.60), channel_id=1, source_target_pairs={{0,1},{1,2},{2,3},{3,4},{4,5},{5,6},{6,7},{8,9},{9,10},{10,11},{11... | collective-permute-start | bytes 4423688 | tf_op jit(solution)/shard_map/ppermute | solution.py:26
  101.6 5.5 collective-permute-start.3
  102.9 4.2 copy-start.5
  116.6 7.8 %copy-start.12 = (bf16[4,4,1441,128]{3,2,1,0:T(8,128)(2,1)}, bf16[4,4,1441,128]{3,2,1,0:T(8,128)(2,1)S(1)}, u32[]{:S(2)}) copy-start(bf16[4,4,1441,128]{3,2,1,0:T(8,128)(2,1)S(1)} %get-tuple-element.52) | copy-start | bytes 17707012
  116.6 25.0 %copy-start.11 = (bf16[4,4,1441,128]{3,2,1,0:T(8,128)(2,1)}, bf16[4,4,1441,128]{3,2,1,0:T(8,128)(2,1)S(1)}, u32[]{:S(2)}) copy-start(bf16[4,4,1441,128]{3,2,1,0:T(8,128)(2,1)S(1)} %get-tuple-element.53) | copy-start | bytes 17707012
  154.3 10.1 %copy-start.23 = (f32[69]{0:T(128)S(1)}, f32[69]{0:T(128)}, u32[]{:S(2)}) copy-start(f32[69]{0:T(128)} %param.13) | copy-start | bytes 832
  154.4 10.1 %copy-start.24 = (f32[69]{0:T(128)S(1)}, f32[69]{0:T(128)}, u32[]{:S(2)}) copy-start(f32[69]{0:T(128)} %param.12) | copy-start | bytes 832
  158.9 10.5 %collective-permute-start.4 = (bf16[4,69,2,360]{3,1,2,0:T(8,128)(2,1)}, bf16[4,69,2,360]{3,1,2,0:T(8,128)(2,1)S(1)}, u32[]{:S(2)}, u32[]{:S(2)}) collective-permute-start(bf16[4,69,2,360]{3,1,2,0:T(8,128)(2,1)} %bitcast.377), channel_id=1, source_target_pairs={{0,8},{8,16},{16,24},{24,0},{1,9},{9,17},{17,25},{25,1},{2,10},{10... | collective-permute-start | bytes 1192328 | tf_op jit(solution)/shard_map/ppermute | solution.py:166
  160.5 18.4 %collective-permute-start.5 = (bf16[4,69,2,360]{3,1,2,0:T(8,128)(2,1)S(1)}, bf16[4,69,2,360]{3,1,2,0:T(8,128)(2,1)}, u32[]{:S(2)}, u32[]{:S(2)}) collective-permute-start(bf16[4,69,2,360]{3,1,2,0:T(8,128)(2,1)S(1)} %bitcast.401), channel_id=1, source_target_pairs={{0,16},{8,24},{16,0},{24,8},{1,17},{9,25},{17,1},{25,9},{2,18},{10... | collective-permute-start | bytes 1192328 | tf_op jit(solution)/shard_map/ppermute | solution.py:166
  163.1 15.8 %collective-permute-start.6 = (bf16[4,69,2,360]{3,1,2,0:T(8,128)(2,1)S(1)}, bf16[4,69,2,360]{3,1,2,0:T(8,128)(2,1)}, u32[]{:S(2)}, u32[]{:S(2)}) collective-permute-start(bf16[4,69,2,360]{3,1,2,0:T(8,128)(2,1)S(1)} %bitcast.399), channel_id=1, source_target_pairs={{0,24},{8,0},{16,8},{24,16},{1,25},{9,1},{17,9},{25,17},{2,26},{10... | collective-permute-start | bytes 1192328 | tf_op jit(solution)/shard_map/ppermute | solution.py:166
  250.6 3.0 copy-start.15
  250.6 3.0 copy-start.18
  295.0 2.9 copy-start.6
  297.7 2.6 slice-start.2
  297.9 3.0 slice-start.3
  297.9 4.3 slice-start.4
  300.8 1.9 slice-start.5
  307.2 37.2 %collective-permute-start.7 = (bf16[4,69,1,1440]{3,0,2,1:T(4,128)(2,1)S(1)}, bf16[4,69,1,1440]{3,0,2,1:T(4,128)(2,1)S(1)}, u32[]{:S(2)}, u32[]{:S(2)}) collective-permute-start(bf16[4,69,1,1440]{3,0,2,1:T(4,128)(2,1)S(1)} %copy.40), channel_id=1, source_target_pairs={{0,1},{1,2},{2,3},{3,4},{4,5},{5,6},{6,7},{8,9},{9,10},{10,11},{11... | collective-permute-start | bytes 2384648 | tf_op jit(solution)/shard_map/ppermute | solution.py:26
  335.6 40.1 %collective-permute-start.8 = (bf16[4,69,1,1440]{3,0,2,1:T(4,128)(2,1)S(1)}, bf16[4,69,1,1440]{3,0,2,1:T(4,128)(2,1)S(1)}, u32[]{:S(2)}, u32[]{:S(2)}) collective-permute-start(bf16[4,69,1,1440]{3,0,2,1:T(4,128)(2,1)S(1)} %copy.41), channel_id=1, source_target_pairs={{1,0},{2,1},{3,2},{4,3},{5,4},{6,5},{7,6},{9,8},{10,9},{11,10},{12... | collective-permute-start | bytes 2384648 | tf_op jit(solution)/shard_map/ppermute | solution.py:28
  339.4 1.4 copy-start.20
  340.8 3.7 copy-start.22
  376.0 16.8 %copy-start.7 = (bf16[4,69,4,1440]{3,1,2,0:T(8,128)(2,1)}, bf16[4,69,4,1440]{3,1,2,0:T(8,128)(2,1)S(1)}, u32[]{:S(2)}) copy-start(bf16[4,69,4,1440]{3,1,2,0:T(8,128)(2,1)S(1)} %get-tuple-element.78) | copy-start | bytes 9538564
  425.7 3.9 copy-start.3
  425.7 8.5 %slice-start = ((s8[5898240]{0:T(1024)(128)(4,1)}), s8[4194304]{0:T(1024)(128)(4,1)S(1)}, s32[]{:S(2)}) async-start(s8[5898240]{0:T(1024)(128)(4,1)} %bitcast.385), calls=%async_computation.2 | async-start | bytes 8388608
  429.6 4.6 slice-start.1
  435.3 1.8 copy-start.10
  437.1 21.9 %slice-start.6 = ((s8[4423680]{0:T(1024)(128)(4,1)}), s8[4194304]{0:T(1024)(128)(4,1)S(1)}, s32[]{:S(2)}) async-start(s8[4423680]{0:T(1024)(128)(4,1)} %bitcast.391), calls=%async_computation.8 | async-start | bytes 8388608
  438.2 20.9 %slice-start.7 = ((s8[4423680]{0:T(1024)(128)(4,1)}), s8[229376]{0:T(1024)(128)(4,1)S(1)}, s32[]{:S(2)}) async-start(s8[4423680]{0:T(1024)(128)(4,1)} %bitcast.391), calls=%async_computation.9 | async-start | bytes 458752
  440.3 153.3 %collective-permute-start.10 = (bf16[4,1,1440,128]{3,2,1,0:T(8,128)(2,1)}, bf16[4,1,1440,128]{3,2,1,0:T(8,128)(2,1)S(1)}, u32[]{:S(2)}, u32[]{:S(2)}) collective-permute-start(bf16[4,1,1440,128]{3,2,1,0:T(8,128)(2,1)} %get-tuple-element.58), channel_id=1, source_target_pairs={{1,0},{2,1},{3,2},{4,3},{5,4},{6,5},{7,6},{9,8},{10,9},{11,10},{12... | collective-permute-start | bytes 4423688 | tf_op jit(solution)/shard_map/ppermute | solution.py:28
  441.6 152.0 %collective-permute-start.9 = (bf16[4,1,1440,128]{3,2,1,0:T(8,128)(2,1)}, bf16[4,1,1440,128]{3,2,1,0:T(8,128)(2,1)}, u32[]{:S(2)}, u32[]{:S(2)}) collective-permute-start(bf16[4,1,1440,128]{3,2,1,0:T(8,128)(2,1)} %get-tuple-element.59), channel_id=1, source_target_pairs={{0,1},{1,2},{2,3},{3,4},{4,5},{5,6},{6,7},{8,9},{9,10},{10,11},{11... | collective-permute-start | bytes 4423688 | tf_op jit(solution)/shard_map/ppermute | solution.py:26
  460.1 1.9 copy-start.17
  461.1 0.8 copy-start.21
  601.3 4.3 copy-start.8
  616.1 3.5 copy-start.4
  627.9 19.4 %copy-start.1 = (f32[69,2,1440]{2,1,0:T(2,128)S(1)}, f32[69,2,1440]{2,1,0:T(2,128)}, u32[]{:S(2)}) copy-start(f32[69,2,1440]{2,1,0:T(2,128)} %param.11) | copy-start | bytes 2384644
Sparse Core Ops, SparseCore 0:
  462.1 127.8 all-reduce.2
